TPU v7x, 512 devices: a whole 4x4x16 slice. The times are simulated.
512 devices in a mesh: rep: 16 (over x, z_lo), mp: 32 (over z_hi, y, core).
Axes of the slice: x: 4, y: 4, z: 16 (z_hi: 4, z_lo: 4; z = z_hi * 4 + z_lo), core: 2. Of those that a mesh axis runs over, the one named last changes fastest.
Arguments:
- dense_feats: bfloat16 [65536, 13], P(('rep', 'mp')), may hold values from -6 to 6
- bag_counts: int32 [65536, 32, 64], P('rep', 'mp'), may hold values from 0 to 2
- emb_rows: bfloat16 [32, 64, 256], P('mp'), may hold values from -0.625 to 0.625
- v_emb: bfloat16 [8192, 256], P('mp'), may hold values from -0.0625 to 0.0625
- u_emb: bfloat16 [256, 8192], P(None, 'mp'), may hold values from -0.375 to 0.375
- b_emb: bfloat16 [8192], P('mp'), may hold values from -3 to 3
- v_bot: bfloat16 [256, 256], replicated, may hold values from -0.375 to 0.375
- u_bot: bfloat16 [256, 256], replicated, may hold values from -0.375 to 0.375
- b_bot: bfloat16 [256], replicated, may hold values from -3 to 3
- w_first: bfloat16 [13, 1024], replicated, may hold values from -1.75 to 1.75
- b_first: bfloat16 [1024], replicated, may hold values from -3 to 3
- w_second: bfloat16 [1024, 256], replicated, may hold values from -0.1875 to 0.1875
- b_second: bfloat16 [256], replicated, may hold values from -3 to 3
- cot_cross: bfloat16 [65536, 8192], P(('rep', 'mp')), may hold values from -24 to 24
- cot_bottom: bfloat16 [65536, 256], P(('rep', 'mp')), may hold values from -6 to 6
Outputs:
- cross_emb: bfloat16 [65536, 8192], P(('rep', 'mp'))
- cross_bot: bfloat16 [65536, 256], P(('rep', 'mp'))
- grad_table: bfloat16 [32, 64, 256], P('mp')
- grad_v_emb: bfloat16 [8192, 256], P('mp')
- grad_u_emb: bfloat16 [256, 8192], P(None, 'mp')
- grad_b_emb: bfloat16 [8192], P('mp')
- grad_v_bot: bfloat16 [256, 256], replicated
- grad_u_bot: bfloat16 [256, 256], replicated
- grad_b_bot: bfloat16 [256], replicated
- grad_w_first: bfloat16 [13, 1024], replicated
- grad_b_first: bfloat16 [1024], replicated
- grad_w_second: bfloat16 [1024, 256], replicated
- grad_b_second: bfloat16 [256], replicated
Inputs may be any that keep to these rules, and one draw needn't show every extreme that they name: bag_counts[s, t, j] is how often row j of table t occurs in the bag of sample s.
All inputs are finite; a program needn't handle non-finite values.
Results may differ from a plain program's by a relative error of at most 0.029.
Values may be sent and summed in bfloat16 or wider, within the bound.
A program may use at most 64 MiB of HBM per device.

v0:
```python
import math

import jax
import jax.numpy as jnp
from jax import lax
from jax.sharding import PartitionSpec as P


def silu_slope(inputs):
    gate_value = jax.nn.sigmoid(inputs)
    return gate_value * (1.0 + inputs * (1.0 - gate_value))


def contract_rows(left_side, right_side):
    return lax.dot_general(
        left_side, right_side, (((0,), (0,)), ((), ())), preferred_element_type=jnp.float32
    )


def contract_cols(left_side, right_side):
    return lax.dot_general(
        left_side, right_side, (((1,), (1,)), ((), ())), preferred_element_type=jnp.float32
    )


def local(
    dense_feats,
    bag_counts,
    emb_rows,
    v_emb,
    u_emb,
    b_emb,
    v_bot,
    u_bot,
    b_bot,
    w_first,
    b_first,
    w_second,
    b_second,
    cot_cross,
    cot_bottom,
):
    group_size = lax.axis_size("mp")
    own_rows = dense_feats.shape[0]
    first_row = lax.axis_index("mp") * own_rows
    grad_scale = 1.0 / math.sqrt(own_rows * group_size * lax.axis_size("rep"))
    counts = bag_counts[:, 0, :].astype(jnp.bfloat16)
    pooled = jnp.dot(counts, emb_rows[0], preferred_element_type=jnp.float32).astype(jnp.bfloat16)
    partial_value = jnp.dot(pooled, v_emb, preferred_element_type=jnp.float32)
    first_pre = jnp.dot(dense_feats, w_first, preferred_element_type=jnp.float32) + b_first.astype(
        jnp.float32
    )
    first_act = jax.nn.silu(first_pre).astype(jnp.bfloat16)
    second_pre = jnp.dot(first_act, w_second, preferred_element_type=jnp.float32) + b_second.astype(
        jnp.float32
    )
    bottom = jax.nn.silu(second_pre).astype(jnp.bfloat16)
    own_part = lax.dynamic_slice_in_dim(partial_value, first_row, own_rows, 0) + jnp.dot(
        bottom, v_bot, preferred_element_type=jnp.float32
    )
    partial_value = lax.dynamic_update_slice_in_dim(partial_value, own_part, first_row, 0)
    low_rank = lax.psum(partial_value.astype(jnp.bfloat16), "mp")
    lift_emb = jnp.dot(low_rank, u_emb, preferred_element_type=jnp.float32) + b_emb.astype(
        jnp.float32
    )
    pooled_full = pooled.astype(jnp.float32)
    cross_local = (pooled_full * (lift_emb + 1.0)).astype(jnp.bfloat16)
    cross_emb = lax.all_to_all(cross_local, "mp", split_axis=0, concat_axis=1, tiled=True)
    own_low = lax.dynamic_slice_in_dim(low_rank, first_row, own_rows, 0)
    lift_bottom = jnp.dot(own_low, u_bot, preferred_element_type=jnp.float32) + b_bot.astype(
        jnp.float32
    )
    bottom_full = bottom.astype(jnp.float32)
    cross_bot = (bottom_full * (lift_bottom + 1.0)).astype(jnp.bfloat16)
    cot_rows = lax.all_to_all(cot_cross, "mp", split_axis=1, concat_axis=0, tiled=True).astype(
        jnp.float32
    )
    d_lift = cot_rows * pooled_full
    d_lift_round = d_lift.astype(jnp.bfloat16)
    own_back = lax.psum_scatter(
        contract_cols(d_lift_round, u_emb).astype(jnp.bfloat16),
        "mp",
        scatter_dimension=0,
        tiled=True,
    ).astype(jnp.float32)
    cot_low = cot_bottom.astype(jnp.float32)
    d_bottom_lift = cot_low * bottom_full
    d_bottom_round = d_bottom_lift.astype(jnp.bfloat16)
    own_d_low = (own_back + contract_cols(d_bottom_round, u_bot)).astype(jnp.bfloat16)
    d_low = lax.all_gather(own_d_low, "mp", axis=0, tiled=True)
    d_pooled = (cot_rows * (lift_emb + 1.0) + contract_cols(d_low, v_emb)).astype(jnp.bfloat16)
    grad_table = grad_scale * contract_rows(counts, d_pooled)
    grad_v = grad_scale * contract_rows(pooled, d_low)
    grad_u = grad_scale * contract_rows(low_rank, d_lift_round)
    grad_b = grad_scale * jnp.sum(d_lift, axis=0)
    d_bottom = cot_low * (lift_bottom + 1.0) + contract_cols(own_d_low, v_bot)
    grad_vb = grad_scale * contract_rows(bottom, own_d_low)
    grad_ub = grad_scale * contract_rows(own_low, d_bottom_round)
    grad_bb = grad_scale * jnp.sum(d_bottom_lift, axis=0)
    d_second = d_bottom * silu_slope(second_pre)
    d_second_round = d_second.astype(jnp.bfloat16)
    grad_ws = grad_scale * contract_rows(first_act, d_second_round)
    grad_bs = grad_scale * jnp.sum(d_second, axis=0)
    d_first = contract_cols(d_second_round, w_second) * silu_slope(first_pre)
    d_first_round = d_first.astype(jnp.bfloat16)
    grad_wf = grad_scale * contract_rows(dense_feats, d_first_round)
    grad_bf = grad_scale * jnp.sum(d_first, axis=0)
    dense_sums = lax.psum(
        (grad_wf, grad_bf, grad_ws, grad_bs, grad_vb, grad_ub, grad_bb), ("rep", "mp")
    )
    table_sums = (
        lax.psum(grad_table.astype(jnp.bfloat16), "rep").astype(jnp.float32),
        lax.psum(grad_v.astype(jnp.bfloat16), "rep").astype(jnp.float32),
        lax.psum(grad_u.astype(jnp.bfloat16), "rep").astype(jnp.float32),
        lax.psum(grad_b.astype(jnp.bfloat16), "rep").astype(jnp.float32),
    )
    return (
        cross_emb,
        cross_bot,
        table_sums[0][None].astype(jnp.bfloat16),
        table_sums[1].astype(jnp.bfloat16),
        table_sums[2].astype(jnp.bfloat16),
        table_sums[3].astype(jnp.bfloat16),
        dense_sums[4].astype(jnp.bfloat16),
        dense_sums[5].astype(jnp.bfloat16),
        dense_sums[6].astype(jnp.bfloat16),
        dense_sums[0].astype(jnp.bfloat16),
        dense_sums[1].astype(jnp.bfloat16),
        dense_sums[2].astype(jnp.bfloat16),
        dense_sums[3].astype(jnp.bfloat16),
    )


def solution(mesh):
    return jax.shard_map(
        local,
        mesh=mesh,
        in_specs=(
            P(("rep", "mp"), None),
            P("rep", "mp", None),
            P("mp", None, None),
            P("mp", None),
            P(None, "mp"),
            P("mp"),
            P(),
            P(),
            P(),
            P(),
            P(),
            P(),
            P(),
            P(("rep", "mp"), None),
            P(("rep", "mp"), None),
        ),
        out_specs=(
            P(("rep", "mp"), None),
            P(("rep", "mp"), None),
            P("mp", None, None),
            P("mp", None),
            P(None, "mp"),
            P("mp"),
            P(),
            P(),
            P(),
            P(),
            P(),
            P(),
            P(),
        ),
        check_vma=False,
    )
```

profile of v0, /device:TPU:8, one launch (start us, length us, event | category | flops | bytes accessed | tf_op | source)
XLA Modules:
  0.0 923.8 jit_solution(9754976400988497330)
XLA Ops:
  7.2 3.2 copy.33
  10.4 18.5 %all-to-all-start.1 = ((bf16[128,32,256]{2,0,1:T(8,128)(2,1)}), bf16[128,32,256]{2,0,1:T(8,128)(2,1)}, u32[]{:S(2)}, u32[]{:S(2)}) async-start(bf16[128,32,256]{2,0,1:T(8,128)(2,1)} %bitcast.58), calls=%async_computation.1 | async-start | bytes 4194304 | tf_op jit(solution)/shard_map/all_to_all | solution.py:75
  30.2 1.0 fusion.22
  31.1 2.0 convolution_convert_fusion.1
  34.2 1.5 convert_element_type.134
  36.4 399.7 %all-reduce.7.cloned.1.call-done = bf16[4096,256]{1,0:T(8,128)(2,1)} async-done(((bf16[4096,256]{1,0:T(8,128)(2,1)}), bf16[4096,256]{1,0:T(8,128)(2,1)}) %all-reduce.7.cloned.1.call-update) | async-done | bytes 2097168 | tf_op jit(solution)/shard_map/psum | solution.py:62
  436.1 6.4 bitcast_multiply_fusion
  442.6 1.3 copy-done.1
  443.9 2.1 convolution_convert_fusion
  446.1 21.6 %all-to-all-start = ((bf16[32,128,256]{2,1,0:T(8,128)(2,1)}), bf16[32,128,256]{2,1,0:T(8,128)(2,1)}, u32[]{:S(2)}, u32[]{:S(2)}) async-start(bf16[32,128,256]{2,1,0:T(8,128)(2,1)} %bitcast.59), calls=%async_computation | async-start | bytes 4194304 | tf_op jit(solution)/shard_map/all_to_all | solution.py:68
  467.7 151.9 %reduce-scatter.2.cloned.1.call-done = bf16[128,256]{1,0:T(8,128)(2,1)} async-done(((bf16[4096,256]{1,0:T(8,128)(2,1)}), bf16[128,256]{1,0:T(8,128)(2,1)}) %reduce-scatter.2.cloned.1.call-update) | async-done | bytes 65552 | tf_op jit(solution)/shard_map/reduce_scatter | solution.py:80
  619.7 1.7 fusion.11
  621.4 1.1 convolution_multiply_fusion.2
  622.5 1.6 fusion.21
  624.2 3.7 fusion.7
  628.9 1.4 convolution_multiply_fusion
  630.3 114.5 %all-reduce.10 = (bf16[256,256]{1,0:T(8,128)(2,1)}, bf16[256,256]{1,0:T(8,128)(2,1)}, bf16[256]{0:T(256)(128)(2,1)}, bf16[13,1024]{1,0:T(8,128)(2,1)}, bf16[1024...) all-reduce(f32[256,256]{1,0:T(8,128)S(1)} %convolution_multiply_fus, ...), channel_id=1, replica_groups=mesh['rep'=16,'mp'=32] {'rep','mp'}, use_global_device_ids=true, to_apply=%region_7.8 | all-reduce | flops 408064 | bytes 2448384 | tf_op jit(solution)/shard_map/psum | solution.py:108
  744.8 3.0 fusion.6
  747.8 4.5 fusion.15
  752.3 78.6 %all-reduce.1 = (bf16[1,64,256]{2,1,0:T(8,128)(2,1)}, bf16[256]{0:T(256)(128)(2,1)}) all-reduce(bf16[1,64,256]{2,1,0:T(8,128)(2,1)S(1)} %fusion.15, bf16[256]{0:T(256)(128)(2,1)S(1)} %multiply_convert_fusion.2), channel_id=1, replica_groups=mesh['rep'=16,'mp'=32] {'rep'}, use_global_device_ids=true, to_apply=%region_2.3 | all-reduce | flops 16640 | bytes 66560 | tf_op jit(solution)/shard_map/psum | solution.py:112
  830.9 3.1 copy.31
  834.0 80.1 %all-reduce.9.cloned.1.call-done = (bf16[256,256]{1,0:T(8,128)(2,1)}, bf16[256,256]{1,0:T(8,128)(2,1)}) async-done(((bf16[256,256]{1,0:T(8,128)(2,1)}, bf16[256,256]{1,0:T(8,128)(2,1)}), (bf16[256,256]{1,0:T(8,128)(2,1)}, bf16[256,256]{1,0:T(8,128)(2,1)})) %all-reduce.9.cloned.1.call-update) | async-done | bytes 262160 | tf_op jit(solution)/shard_map/psum | solution.py:113
  914.1 1.6 copy.52
  915.7 1.6 copy.53
  (63 shorter events, 4.0 us)
Async XLA Ops:
  7.2 23.0 %copy-start = (bf16[1024,256]{1,0:T(8,128)(2,1)S(1)}, bf16[1024,256]{1,0:T(8,128)(2,1)}, u32[]{:S(2)}) copy-start(bf16[1024,256]{1,0:T(8,128)(2,1)} %param.26) | copy-start | bytes 1572868
  10.4 18.6 %copy-start.15 = (bf16[256]{0:T(256)(128)(2,1)S(1)}, bf16[256]{0:T(256)(128)(2,1)}, u32[]{:S(2)}) copy-start(bf16[256]{0:T(256)(128)(2,1)} %param.27) | copy-start | bytes 1540
  10.4 18.6 %copy-start.14 = (bf16[1024]{0:T(1024)(128)(2,1)S(1)}, bf16[1024]{0:T(1024)(128)(2,1)}, u32[]{:S(2)}) copy-start(bf16[1024]{0:T(1024)(128)(2,1)} %param.25) | copy-start | bytes 6148
  10.4 18.7 %copy-start.12 = (bf16[13,1024]{1,0:T(8,128)(2,1)S(1)}, bf16[13,1024]{1,0:T(8,128)(2,1)}, u32[]{:S(2)}) copy-start(bf16[13,1024]{1,0:T(8,128)(2,1)} %param.24) | copy-start | bytes 79876
  10.4 18.7 %copy-start.13 = (bf16[128,13]{0,1:T(8,128)(2,1)S(1)}, bf16[128,13]{0,1:T(8,128)(2,1)}, u32[]{:S(2)}) copy-start(bf16[128,13]{0,1:T(8,128)(2,1)} %param.15) | copy-start | bytes 9988
  10.4 19.7 %copy-start.8 = (bf16[128,256]{1,0:T(8,128)(2,1)S(1)}, bf16[128,256]{1,0:T(8,128)(2,1)}, u32[]{:S(2)}) copy-start(bf16[128,256]{1,0:T(8,128)(2,1)} %param.29) | copy-start | bytes 196612
  10.4 425.7 %all-to-all-start.1 = ((bf16[128,32,256]{2,0,1:T(8,128)(2,1)}), bf16[128,32,256]{2,0,1:T(8,128)(2,1)}, u32[]{:S(2)}, u32[]{:S(2)}) async-start(bf16[128,32,256]{2,0,1:T(8,128)(2,1)} %bitcast.58), calls=%async_computation.1 | async-start | bytes 4194304 | tf_op jit(solution)/shard_map/all_to_all | solution.py:75
  29.0 2.1 copy-start.11
  29.0 407.2 %all-reduce.7.cloned.1.call-start = ((), (), s32[]{:S(2)}) async-start(), calls=%async_computation.3 | async-start | bytes 4194304 | tf_op jit(solution)/shard_map/psum | solution.py:62
  29.4 0.8 copy-start.5
  31.1 2.0 copy-start.4
  33.1 0.9 copy-start.9
  35.8 400.4 %copy-start.3 = (bf16[256,256]{1,0:T(8,128)(2,1)S(1)}, bf16[256,256]{1,0:T(8,128)(2,1)}, u32[]{:S(2)}) copy-start(bf16[256,256]{1,0:T(8,128)(2,1)} %param.19) | copy-start | bytes 393220
  35.8 583.9 %reduce-scatter.2.cloned.1.call-start = ((), (), s32[]{:S(2)}) async-start(), calls=%async_computation.4 | async-start | bytes 2162688 | tf_op jit(solution)/shard_map/reduce_scatter | solution.py:80
  442.6 1.3 copy-start.1
  446.0 173.6 %copy-start.7 = (bf16[256,256]{1,0:T(8,128)(2,1)S(1)}, bf16[256,256]{1,0:T(8,128)(2,1)}, u32[]{:S(2)}) copy-start(bf16[256,256]{1,0:T(8,128)(2,1)} %param.22) | copy-start | bytes 393220
  446.1 175.3 %copy-start.17 = (bf16[256]{0:T(256)(128)(2,1)S(1)}, bf16[256]{0:T(256)(128)(2,1)}, u32[]{:S(2)}) copy-start(bf16[256]{0:T(256)(128)(2,1)} %param.23) | copy-start | bytes 1540
  446.1 384.9 %all-to-all-start = ((bf16[32,128,256]{2,1,0:T(8,128)(2,1)}), bf16[32,128,256]{2,1,0:T(8,128)(2,1)}, u32[]{:S(2)}, u32[]{:S(2)}) async-start(bf16[32,128,256]{2,1,0:T(8,128)(2,1)} %bitcast.59), calls=%async_computation | async-start | bytes 4194304 | tf_op jit(solution)/shard_map/all_to_all | solution.py:68
  467.7 277.1 %all-gather.2.cloned.1.call-start = ((), (), s32[]{:S(2)}) async-start(), calls=%async_computation.5 | async-start | bytes 2162688 | tf_op jit(solution)/shard_map/all_gather | solution.py:90
  621.4 292.8 %all-reduce.9.cloned.1.call-start = ((), (), s32[]{:S(2)}) async-start(), calls=%async_computation.6 | async-start | bytes 524288 | tf_op jit(solution)/shard_map/psum | solution.py:113
  624.2 3.7 copy-start.2
  624.2 4.0 copy-start.10
  624.2 4.0 copy-start.18
  624.2 4.2 copy-start.6
  (1 other events, 0.7 us)
Sparse Core Ops, SparseCore 0:
  35.9 400.1 all-reduce.6
  446.2 173.4 reduce-scatter.1
  623.8 74.0 all-gather.1
  747.9 166.1 all-reduce.8
where the time goes:
time: 924 us
  waiting for transfers between devices  632 us (68%)
  blocking collectives  193 us (21%)
  starting transfers between devices  40.3 us (4%)
  matrix products  30.5 us (3%)
  between operations  14.1 us (2%)
  local copies, waits for them, and re-layouts  12.5 us (1%)
    psum x1, waiting for transfers between devices, local(): low_rank = lax.psum(partial_value.astype(jnp.bfloat16), 'mp')  400 us
    reduce_scatter x1, waiting for transfers between devices, local(): lax.psum_scatter(contract_cols(d_lift_round, u_emb).astype(jnp.bfloat16),...  152 us
    psum x1, blocking collectives, local(): lax.psum((grad_wf, grad_bf, grad_ws, grad_bs, grad_vb, grad_ub, grad_bb),...  115 us
    psum x1, waiting for transfers between devices, local(): lax.psum(grad_v.astype(jnp.bfloat16), 'rep').astype(jnp.float32)  80.1 us
    psum x1, blocking collectives, local(): lax.psum(grad_table.astype(jnp.bfloat16), 'rep').astype(jnp.float32)  78.6 us
    all_to_all x1, starting transfers between devices, local(): lax.all_to_all(cross_local, 'mp', split_axis=0, concat_axis=1, tiled=True)  21.6 us
    all_to_all x1, starting transfers between devices, local(): lax.all_to_all(cot_cross, 'mp', split_axis=1, concat_axis=0, tiled=True)  18.5 us
  transfers between devices with their start and end apart: 6, of which 3 were waited for; matrix products, arithmetic and copies ran while one was open for 3% of the time, Pallas kernels for 0%

commit v1 on v0

v1 whole, which is shorter than its diff:
```python
import math

import jax
import jax.numpy as jnp
from jax import lax
from jax.sharding import PartitionSpec as P


def silu_slope(inputs):
    gate_value = jax.nn.sigmoid(inputs)
    return gate_value * (1.0 + inputs * (1.0 - gate_value))


def contract_rows(left_side, right_side):
    return lax.dot_general(
        left_side, right_side, (((0,), (0,)), ((), ())), preferred_element_type=jnp.float32
    )


def contract_cols(left_side, right_side):
    return lax.dot_general(
        left_side, right_side, (((1,), (1,)), ((), ())), preferred_element_type=jnp.float32
    )


def local(
    dense_feats,
    bag_counts,
    emb_rows,
    v_emb,
    u_emb,
    b_emb,
    v_bot,
    u_bot,
    b_bot,
    w_first,
    b_first,
    w_second,
    b_second,
    cot_cross,
    cot_bottom,
):
    tables = lax.axis_size("mp")
    replicas = lax.axis_size("rep")
    own_rows = dense_feats.shape[0]
    table_rows, width = emb_rows.shape[1:]
    rank = v_emb.shape[1]
    share = width // replicas
    grad_scale = 1.0 / math.sqrt(own_rows * tables * replicas)

    first = lax.axis_index("rep") * share
    pad = -(table_rows + 1) % 128
    packed = jnp.concatenate(
        [
            v_emb,
            u_emb.T,
            emb_rows[0].T,
            b_emb[:, None],
            jnp.zeros((width, pad), jnp.bfloat16),
        ],
        axis=1,
    )
    packed = lax.dynamic_slice_in_dim(packed, first, share, 0)
    packed = lax.all_gather(packed, ("mp", "rep"), axis=0, tiled=True)

    counts = bag_counts[:, 0, :].astype(jnp.bfloat16)
    counts = jnp.swapaxes(counts.reshape(tables, own_rows, table_rows), 1, 2)
    counts = lax.all_to_all(counts, "mp", split_axis=0, concat_axis=0, tiled=True)

    first_pre = jnp.dot(dense_feats, w_first, preferred_element_type=jnp.float32) + b_first.astype(
        jnp.float32
    )
    first_act = jax.nn.silu(first_pre).astype(jnp.bfloat16)
    second_pre = jnp.dot(first_act, w_second, preferred_element_type=jnp.float32) + b_second.astype(
        jnp.float32
    )
    bottom = jax.nn.silu(second_pre).astype(jnp.bfloat16)

    v_all = packed[:, :rank]
    u_all = packed[:, rank : 2 * rank]
    emb_all = packed[:, 2 * rank : 2 * rank + table_rows].reshape(tables, width, table_rows)
    b_all = packed[:, 2 * rank + table_rows].reshape(1, tables * width).astype(jnp.float32)

    pooled = lax.dot_general(
        counts, emb_all, (((1,), (2,)), ((0,), (0,))), preferred_element_type=jnp.float32
    ).astype(jnp.bfloat16)
    pooled = jnp.swapaxes(pooled, 0, 1).reshape(own_rows, tables * width)
    low_rank = (
        jnp.dot(pooled, v_all, preferred_element_type=jnp.float32)
        + jnp.dot(bottom, v_bot, preferred_element_type=jnp.float32)
    ).astype(jnp.bfloat16)
    lift_emb = contract_cols(low_rank, u_all) + b_all
    pooled_full = pooled.astype(jnp.float32)
    cross_emb = (pooled_full * (lift_emb + 1.0)).astype(jnp.bfloat16)
    lift_bottom = jnp.dot(low_rank, u_bot, preferred_element_type=jnp.float32) + b_bot.astype(
        jnp.float32
    )
    bottom_full = bottom.astype(jnp.float32)
    cross_bot = (bottom_full * (lift_bottom + 1.0)).astype(jnp.bfloat16)
    cot_rows = cot_cross.astype(jnp.float32)
    d_lift = cot_rows * pooled_full
    d_lift_round = d_lift.astype(jnp.bfloat16)
    cot_low = cot_bottom.astype(jnp.float32)
    d_bottom_lift = cot_low * bottom_full
    d_bottom_round = d_bottom_lift.astype(jnp.bfloat16)
    d_low = (
        jnp.dot(d_lift_round, u_all, preferred_element_type=jnp.float32)
        + contract_cols(d_bottom_round, u_bot)
    ).astype(jnp.bfloat16)
    d_pooled = (cot_rows * (lift_emb + 1.0) + contract_cols(d_low, v_all)).astype(jnp.bfloat16)
    d_tables = jnp.swapaxes(d_pooled.reshape(own_rows, tables, width), 0, 1)
    grad_table = lax.dot_general(
        d_tables, counts, (((1,), (2,)), ((0,), (0,))), preferred_element_type=jnp.float32
    ).reshape(tables * width, table_rows)
    grad_v = contract_rows(pooled, d_low)
    grad_u = contract_rows(d_lift_round, low_rank)
    grad_b = jnp.sum(d_lift, axis=0)
    grads = jnp.concatenate(
        [
            grad_v.astype(jnp.bfloat16),
            grad_u.astype(jnp.bfloat16),
            grad_table.astype(jnp.bfloat16),
            grad_b.astype(jnp.bfloat16)[:, None],
            jnp.zeros((tables * width, pad), jnp.bfloat16),
        ],
        axis=1,
    )
    columns = grads.shape[1]
    grads = jnp.swapaxes(grads.reshape(tables, replicas, share, columns), 0, 1)
    grads = lax.psum_scatter(
        grads.reshape(replicas * tables * share, columns), "rep", scatter_dimension=0, tiled=True
    )
    grads = lax.psum_scatter(
        grads.astype(jnp.float32) * grad_scale, "mp", scatter_dimension=0, tiled=True
    )
    grads = lax.optimization_barrier(grads).astype(jnp.bfloat16)
    grads = lax.all_gather(grads, "rep", axis=0, tiled=True)

    d_bottom = cot_low * (lift_bottom + 1.0) + contract_cols(d_low, v_bot)
    grad_vb = grad_scale * contract_rows(bottom, d_low)
    grad_ub = grad_scale * contract_rows(low_rank, d_bottom_round)
    grad_bb = grad_scale * jnp.sum(d_bottom_lift, axis=0)
    d_second = d_bottom * silu_slope(second_pre)
    d_second_round = d_second.astype(jnp.bfloat16)
    grad_ws = grad_scale * contract_rows(first_act, d_second_round)
    grad_bs = grad_scale * jnp.sum(d_second, axis=0)
    d_first = contract_cols(d_second_round, w_second) * silu_slope(first_pre)
    d_first_round = d_first.astype(jnp.bfloat16)
    grad_wf = grad_scale * contract_rows(dense_feats, d_first_round)
    grad_bf = grad_scale * jnp.sum(d_first, axis=0)
    dense_sums = lax.psum(
        (grad_wf, grad_bf, grad_ws, grad_bs, grad_vb, grad_ub, grad_bb), ("rep", "mp")
    )
    return (
        cross_emb,
        cross_bot,
        grads[:, 2 * rank : 2 * rank + table_rows].T[None],
        grads[:, :rank],
        grads[:, rank : 2 * rank].T,
        grads[:, 2 * rank + table_rows],
        dense_sums[4].astype(jnp.bfloat16),
        dense_sums[5].astype(jnp.bfloat16),
        dense_sums[6].astype(jnp.bfloat16),
        dense_sums[0].astype(jnp.bfloat16),
        dense_sums[1].astype(jnp.bfloat16),
        dense_sums[2].astype(jnp.bfloat16),
        dense_sums[3].astype(jnp.bfloat16),
    )


def solution(mesh):
    return jax.shard_map(
        local,
        mesh=mesh,
        in_specs=(
            P(("rep", "mp"), None),
            P("rep", "mp", None),
            P("mp", None, None),
            P("mp", None),
            P(None, "mp"),
            P("mp"),
            P(),
            P(),
            P(),
            P(),
            P(),
            P(),
            P(),
            P(("rep", "mp"), None),
            P(("rep", "mp"), None),
        ),
        out_specs=(
            P(("rep", "mp"), None),
            P(("rep", "mp"), None),
            P("mp", None, None),
            P("mp", None),
            P(None, "mp"),
            P("mp"),
            P(),
            P(),
            P(),
            P(),
            P(),
            P(),
            P(),
        ),
        check_vma=False,
    )
```

time: 924 us -> 1930 us (2.09)
  waiting for transfers between devices: 632 us -> 1650 us
  local copies, waits for them, and re-layouts: 12.5 us -> 50.2 us
  blocking collectives: 193 us -> 158 us
  starting transfers between devices: 40.3 us -> 18.7 us
    all_gather x1, waiting for transfers between devices: 0.01 us -> 1390 us  [local(): packed = lax.all_gather(packed, ('mp', 'rep'), axis=0, tiled=True)]
    psum x2 -> x0, waiting for transfers between devices: 480 us -> none  [the longest x1 400 us: local(): low_rank = lax.psum(partial_value.astype(jnp.bfloat16), 'mp')]
    reduce_scatter x1 -> x2, waiting for transfers between devices: 152 us -> 266 us  [the longest x1 266 us: local(): lax.psum_scatter(grads.reshape(replicas * tables * share, columns), 'rep'...]
    psum x1 -> x0, blocking collectives: 78.6 us -> none  [local(): lax.psum(grad_table.astype(jnp.bfloat16), 'rep').astype(jnp.float32)]
    all_gather x0 -> x1, blocking collectives: none -> 44.4 us  [local(): grads = lax.all_gather(grads, 'rep', axis=0, tiled=True)]
    concatenate x0 -> x4, local copies, waits for them, and re-layouts: none -> 27.2 us  [the longest x3 26.2 us: local(): jnp.concatenate([grad_v.astype(jnp.bfloat16), grad_u.astype(jnp.bfloat16)...]
    all_to_all x2 -> x1, starting transfers between devices: 40.1 us -> 18.3 us  [local(): lax.all_to_all(counts, 'mp', split_axis=0, concat_axis=0, tiled=True)]
  transfers between devices with their start and end apart: 6 -> 4, of which waited for: 3 -> 3; matrix products, arithmetic and copies ran while one was open for 3% -> 0% of each run, Pallas kernels for 0% -> 0%
where the time goes in v1:
time: 1930 us
  waiting for transfers between devices  1650 us (85%)
  blocking collectives  158 us (8%)
  local copies, waits for them, and re-layouts  50.2 us (3%)
  matrix products  26 us (1%)
    all_gather x1, waiting for transfers between devices, local(): packed = lax.all_gather(packed, ('mp', 'rep'), axis=0, tiled=True)  1390 us
    reduce_scatter x1, waiting for transfers between devices, local(): lax.psum_scatter(grads.reshape(replicas * tables * share, columns), 'rep'...  266 us
    psum x1, blocking collectives, local(): lax.psum((grad_wf, grad_bf, grad_ws, grad_bs, grad_vb, grad_ub, grad_bb),...  114 us
    all_gather x1, blocking collectives, local(): grads = lax.all_gather(grads, 'rep', axis=0, tiled=True)  44.4 us
  transfers between devices with their start and end apart: 4, of which 3 were waited for; matrix products, arithmetic and copies ran while one was open for 0% of the time, Pallas kernels for 0%

profile of v1, /device:TPU:8, one launch (start us, length us, event | category | flops | bytes accessed | tf_op | source)
XLA Modules:
  0.0 1927.5 jit_solution(6832458507843473368)
XLA Ops:
  14.2 18.3 all-to-all-start
  33.7 1.5 fusion.23
  35.2 1388.3 %all-gather.2.cloned.1.call-done = bf16[8192,640]{1,0:T(8,128)(2,1)} async-done(((bf16[16,640]{1,0:T(8,128)(2,1)}), bf16[8192,640]{1,0:T(8,128)(2,1)}) %all-gather.2.cloned.1.call-update) | async-done | bytes 10485776 | tf_op jit(solution)/shard_map/all_gather | solution.py:64
  1423.6 1.6 slice-done.3
  1425.2 2.0 convolution_convert_fusion.2
  1427.2 2.9 copy.78
  1430.1 3.8 fusion.9
  1434.1 3.4 convolution_convert_fusion
  1437.6 4.0 fusion.5
  1441.8 3.3 convolution_convert_fusion.1
  1445.1 1.4 convert_reduce_fusion
  1446.5 3.0 fusion.3
  1449.5 1.6 fusion.1
  1451.5 1.8 copy.80
  1453.3 2.1 copy.83
  1455.6 4.2 copy.84
  1459.8 4.8 copy.82
  1464.6 2.5 copy.81
  1467.2 1.7 broadcast_in_dim.18
  1468.9 18.8 concatenate.14
  1489.1 265.8 %reduce-scatter.3.cloned.1.call-done = bf16[512,640]{1,0:T(8,128)(2,1)} async-done(((bf16[8192,640]{1,0:T(8,128)(2,1)}), bf16[512,640]{1,0:T(8,128)(2,1)}) %reduce-scatter.3.cloned.1.call-update) | async-done | bytes 655376 | tf_op jit(solution)/shard_map/reduce_scatter | solution.py:130
  1754.9 2.3 convert_multiply_fusion.3
  1758.8 114.1 %all-reduce.2 = (bf16[256,256]{1,0:T(8,128)(2,1)}, bf16[256,256]{1,0:T(8,128)(2,1)}, bf16[256]{0:T(256)(128)(2,1)}, bf16[13,1024]{1,0:T(8,128)(2,1)}, bf16[1024]...) all-reduce(f32[256,256]{1,0:T(8,128)S(1)} %convolution_multiply_fus, ...), channel_id=1, replica_groups=mesh['rep'=16,'mp'=32] {'rep','mp'}, use_global_device_ids=true, to_apply=%region_3.4 | all-reduce | flops 408064 | bytes 2448384 | tf_op jit(solution)/shard_map/psum | solution.py:151
  1873.7 44.4 %all_gather.7 = bf16[256,640]{1,0:T(8,128)(2,1)S(1)} all-gather(bf16[16,640]{1,0:T(8,128)(2,1)S(1)} %convert_element_type.162), channel_id=1, replica_groups=mesh['rep'=16,'mp'=32] {'rep'}, dimensions={0}, use_global_device_ids=true | all-gather | bytes 348160 | tf_op jit(solution)/shard_map/all_gather | solution.py:137
  (84 shorter events, 15.7 us)
Async XLA Ops:
  7.2 26.5 %copy-start = (bf16[1024,256]{1,0:T(8,128)(2,1)S(1)}, bf16[1024,256]{1,0:T(8,128)(2,1)}, u32[]{:S(2)}) copy-start(bf16[1024,256]{1,0:T(8,128)(2,1)} %param.26) | copy-start | bytes 1572868
  7.2 25.4 %copy-start.13 = (bf16[1024]{0:T(1024)(128)(2,1)S(1)}, bf16[1024]{0:T(1024)(128)(2,1)}, u32[]{:S(2)}) copy-start(bf16[1024]{0:T(1024)(128)(2,1)} %param.25) | copy-start | bytes 6148
  7.2 25.4 %copy-start.15 = (bf16[256]{0:T(256)(128)(2,1)S(1)}, bf16[256]{0:T(256)(128)(2,1)}, u32[]{:S(2)}) copy-start(bf16[256]{0:T(256)(128)(2,1)} %param.27) | copy-start | bytes 1540
  7.2 25.4 %copy-start.11 = (bf16[128,13]{0,1:T(8,128)(2,1)S(1)}, bf16[128,13]{0,1:T(8,128)(2,1)}, u32[]{:S(2)}) copy-start(bf16[128,13]{0,1:T(8,128)(2,1)} %param.15) | copy-start | bytes 9988
  7.2 25.4 %copy-start.10 = (bf16[13,1024]{1,0:T(8,128)(2,1)S(1)}, bf16[13,1024]{1,0:T(8,128)(2,1)}, u32[]{:S(2)}) copy-start(bf16[13,1024]{1,0:T(8,128)(2,1)} %param.24) | copy-start | bytes 79876
  7.2 26.5 %copy-start.7 = (bf16[128,256]{1,0:T(8,128)(2,1)S(1)}, bf16[128,256]{1,0:T(8,128)(2,1)}, u32[]{:S(2)}) copy-start(bf16[128,256]{1,0:T(8,128)(2,1)} %param.29) | copy-start | bytes 196612
  7.2 1416.3 %all-gather.2.cloned.1.call-start = ((), (), s32[]{:S(2)}) async-start(), calls=%async_computation.3 | async-start | bytes 10506240 | tf_op jit(solution)/shard_map/all_gather | solution.py:64
  14.2 1409.4 %all-to-all-start = ((bf16[32,64,128]{2,1,0:T(8,128)(2,1)}), bf16[32,64,128]{2,1,0:T(8,128)(2,1)S(1)}, u32[]{:S(2)}, u32[]{:S(2)}) async-start(bf16[32,64,128]{2,1,0:T(8,128)(2,1)} %bitcast.68), calls=%async_computation | async-start | bytes 1048576 | tf_op jit(solution)/shard_map/all_to_all | solution.py:68
  32.5 1722.4 %reduce-scatter.3.cloned.1.call-start = ((), (), s32[]{:S(2)}) async-start(), calls=%async_computation.4 | async-start | bytes 11141120 | tf_op jit(solution)/shard_map/reduce_scatter | solution.py:130
  1423.6 1.6 slice-start.3
  1430.1 3.9 copy-start.8
  1430.1 4.0 copy-start.1
  1434.1 11.0 slice-start
  1434.1 11.0 slice-start.1
  1437.6 4.0 copy-start.4
  1437.6 4.2 copy-start.3
  1437.6 7.5 slice-start.2
  1459.8 4.8 copy-start.2
  1487.7 269.5 %copy-start.9 = (bf16[256,256]{1,0:T(8,128)(2,1)S(1)}, bf16[256,256]{1,0:T(8,128)(2,1)}, u32[]{:S(2)}) copy-start(bf16[256,256]{1,0:T(8,128)(2,1)} %param.21) | copy-start | bytes 393220
  1487.7 269.5 %copy-start.17 = (f32[128,256]{1,0:T(8,128)S(1)}, f32[128,256]{1,0:T(8,128)}, u32[]{:S(2)}) copy-start(f32[128,256]{1,0:T(8,128)} %get-tuple-element.91) | copy-start | bytes 393220
  1487.7 269.8 %copy-start.14 = (f32[256]{0:T(256)S(1)}, f32[256]{0:T(256)}, u32[]{:S(2)}) copy-start(f32[256]{0:T(256)} %get-tuple-element.85) | copy-start | bytes 3076
  1487.7 269.8 %copy-start.6 = (f32[128,1024]{1,0:T(8,128)S(1)}, f32[128,1024]{1,0:T(8,128)}, u32[]{:S(2)}) copy-start(f32[128,1024]{1,0:T(8,128)} %copy-done.5) | copy-start | bytes 1572868
  1487.7 270.1 %copy-start.12 = (bf16[128,13]{0,1:T(8,128)(2,1)S(1)}, bf16[128,13]{0,1:T(8,128)(2,1)}, u32[]{:S(2)}) copy-start(bf16[128,13]{0,1:T(8,128)(2,1)} %param.15) | copy-start | bytes 9988
  1487.7 385.2 %reduce-scatter.5.cloned.1.call-start = ((), (), s32[]{:S(2)}) async-start(), calls=%async_computation.5 | async-start | bytes 1351680 | tf_op jit(solution)/shard_map/reduce_scatter | solution.py:133
  (2 other events, 1.5 us)
Sparse Core Ops, SparseCore 0:
  11.9 1411.6 all-gather.1
  1487.8 267.0 reduce-scatter.2
  1759.3 113.5 reduce-scatter.4

commit v2 on v1

--- a/solution.py
+++ b/solution.py
@@ -61,7 +61,11 @@
         axis=1,
     )
     packed = lax.dynamic_slice_in_dim(packed, first, share, 0)
-    packed = lax.all_gather(packed, ("mp", "rep"), axis=0, tiled=True)
+    columns = packed.shape[1]
+    packed = lax.all_gather(packed, "mp", axis=0, tiled=True)
+    packed = lax.all_gather(packed, "rep", axis=0, tiled=True)
+    packed = jnp.swapaxes(packed.reshape(replicas, tables, share, columns), 0, 1)
+    packed = packed.reshape(tables * width, columns)
 
     counts = bag_counts[:, 0, :].astype(jnp.bfloat16)
     counts = jnp.swapaxes(counts.reshape(tables, own_rows, table_rows), 1, 2)
@@ -125,17 +129,6 @@
         ],
         axis=1,
     )
-    columns = grads.shape[1]
-    grads = jnp.swapaxes(grads.reshape(tables, replicas, share, columns), 0, 1)
-    grads = lax.psum_scatter(
-        grads.reshape(replicas * tables * share, columns), "rep", scatter_dimension=0, tiled=True
-    )
-    grads = lax.psum_scatter(
-        grads.astype(jnp.float32) * grad_scale, "mp", scatter_dimension=0, tiled=True
-    )
-    grads = lax.optimization_barrier(grads).astype(jnp.bfloat16)
-    grads = lax.all_gather(grads, "rep", axis=0, tiled=True)
-
     d_bottom = cot_low * (lift_bottom + 1.0) + contract_cols(d_low, v_bot)
     grad_vb = grad_scale * contract_rows(bottom, d_low)
     grad_ub = grad_scale * contract_rows(low_rank, d_bottom_round)
@@ -148,9 +141,18 @@
     d_first_round = d_first.astype(jnp.bfloat16)
     grad_wf = grad_scale * contract_rows(dense_feats, d_first_round)
     grad_bf = grad_scale * jnp.sum(d_first, axis=0)
-    dense_sums = lax.psum(
-        (grad_wf, grad_bf, grad_ws, grad_bs, grad_vb, grad_ub, grad_bb), ("rep", "mp")
-    )
+    grads = jnp.swapaxes(grads.reshape(tables, replicas, share, columns), 0, 1)
+    grads = grads.reshape(replicas * tables * share, columns)
+    dense = (grad_wf, grad_bf, grad_ws, grad_bs, grad_vb, grad_ub, grad_bb)
+    grads, dense = lax.optimization_barrier((grads, dense))
+    grads = lax.psum_scatter(grads, "rep", scatter_dimension=0, tiled=True)
+    dense_sums = lax.psum(dense, ("rep", "mp"))
+    grads, dense_sums = lax.optimization_barrier((grads, dense_sums))
+    grads = lax.psum_scatter(
+        grads.astype(jnp.float32) * grad_scale, "mp", scatter_dimension=0, tiled=True
+    )
+    grads = lax.optimization_barrier(grads).astype(jnp.bfloat16)
+    grads = lax.all_gather(grads, "rep", axis=0, tiled=True)
     return (
         cross_emb,
         cross_bot,

time: 1930 us -> 812 us (0.42)
  waiting for transfers between devices: 1650 us -> 462 us
  blocking collectives: 158 us -> 227 us
    all_gather x1, waiting for transfers between devices: 1390 us -> 238 us  [local(): packed = lax.all_gather(packed, 'rep', axis=0, tiled=True)]
    reduce_scatter x1, waiting for transfers between devices: 266 us -> 109 us  [local(): grads = lax.psum_scatter(grads, 'rep', scatter_dimension=0, tiled=True)]
    reduce_scatter x1, waiting for transfers between devices: 0.06 us -> 115 us  [local(): lax.psum_scatter(grads.astype(jnp.float32) * grad_scale, 'mp', scatter_di...]
    all_gather x0 -> x1, blocking collectives: none -> 57.4 us  [local(): packed = lax.all_gather(packed, 'mp', axis=0, tiled=True)]
  transfers between devices with their start and end apart: 4 -> 4, of which waited for: 3 -> 3; matrix products, arithmetic and copies ran while one was open for 0% -> 2% of each run, Pallas kernels for 0% -> 0%
where the time goes in v2:
time: 812 us; the launch traced here: 811 us
  waiting for transfers between devices  462 us (57%)
  blocking collectives  227 us (28%)
  local copies, waits for them, and re-layouts  61.7 us (8%)
  matrix products  25.6 us (3%)
  between operations  14.2 us (2%)
  starting transfers between devices  13 us (2%)
    all_gather x1, waiting for transfers between devices, local(): packed = lax.all_gather(packed, 'rep', axis=0, tiled=True)  238 us
    psum x1, blocking collectives, local(): dense_sums = lax.psum(dense, ('rep', 'mp'))  125 us
    reduce_scatter x1, waiting for transfers between devices, local(): lax.psum_scatter(grads.astype(jnp.float32) * grad_scale, 'mp', scatter_di...  115 us
    reduce_scatter x1, waiting for transfers between devices, local(): grads = lax.psum_scatter(grads, 'rep', scatter_dimension=0, tiled=True)  109 us
    all_gather x1, blocking collectives, local(): packed = lax.all_gather(packed, 'mp', axis=0, tiled=True)  57.4 us
    all_gather x1, blocking collectives, local(): grads = lax.all_gather(grads, 'rep', axis=0, tiled=True)  44 us
    concatenate x3, local copies, waits for them, and re-layouts, local(): jnp.concatenate([grad_v.astype(jnp.bfloat16), grad_u.astype(jnp.bfloat16)...  26.2 us
  transfers between devices with their start and end apart: 4, of which 3 were waited for; matrix products, arithmetic and copies ran while one was open for 2% of the time, Pallas kernels for 0%

profile of v2, /device:TPU:8, one launch (start us, length us, event | category | flops | bytes accessed | tf_op | source)
XLA Modules:
  0.0 810.7 jit_solution(15563284094259363290)
XLA Ops:
  11.2 57.4 %all_gather.9 = bf16[512,640]{1,0:T(8,128)(2,1)} all-gather(bf16[16,640]{1,0:T(8,128)(2,1)S(1)} %constant_dynamic-slice_fusion), channel_id=1, replica_groups=mesh['rep'=16,'mp'=32] {'mp'}, dimensions={0}, use_global_device_ids=true | all-gather | bytes 675840 | tf_op jit(solution)/shard_map/all_gather | solution.py:65
  71.0 12.9 %all-to-all-start = ((bf16[32,64,128]{2,1,0:T(8,128)(2,1)}), bf16[32,64,128]{2,1,0:T(8,128)(2,1)S(1)}, u32[]{:S(2)}, u32[]{:S(2)}) async-start(bf16[32,64,128]{2,1,0:T(8,128)(2,1)} %bitcast.72), calls=%async_computation | async-start | bytes 1048576 | tf_op jit(solution)/shard_map/all_to_all | solution.py:72
  86.0 237.6 %all-gather.2.cloned.1.call-done = bf16[8192,640]{1,0:T(8,128)(2,1)} async-done(((bf16[512,640]{1,0:T(8,128)(2,1)}), bf16[8192,640]{1,0:T(8,128)(2,1)}) %all-gather.2.cloned.1.call-update) | async-done | bytes 10485776 | tf_op jit(solution)/shard_map/all_gather | solution.py:66
  323.5 9.6 %copy.52 = bf16[32,16,16,640]{3,2,1,0:T(8,128)(2,1)} copy(bf16[32,16,16,640]{3,2,0,1:T(8,128)(2,1)} %bitcast.87) | data formatting | bytes 20971520 | tf_op jit(solution)/shard_map/transpose | solution.py:67
  333.2 1.7 slice.32
  336.9 3.1 fusion.9
  340.0 3.1 copy.56
  343.1 3.0 convert_reduce_fusion
  346.2 3.7 fusion.5
  350.1 3.4 convolution_convert_fusion
  353.8 3.3 convolution_convert_fusion.1
  361.8 3.0 fusion.3
  366.8 1.8 copy.58
  368.6 2.1 copy.61
  370.9 4.2 copy.62
  375.1 4.8 copy.60
  379.9 2.5 copy.59
  382.6 1.7 broadcast_in_dim.18
  384.3 18.8 %concatenate.14 = bf16[32,16,16,640]{3,2,0,1:T(8,128)(2,1)} concatenate(bf16[32,16,16,256]{3,2,0,1:T(8,128)(2,1)} %copy.59, bf16[32,16,16,256]{3,2,0,1:T(8,128)(2,1)} %copy.60, bf16[32,16,16,64]{3,2,0,1:T(8,128)(2,1)S(1)} %copy.61, bf16[32,16,16,1]{3,2,0,1:T(8,128)(2,1)} %copy.62, bf16[32,16,16,63]{3,2,0,1:T(8,128)(2,1)} %broadcast_in_dim.18), dimensions={3} | concatenate | bytes 20971520 | tf_op jit(solution)/shard_map/concatenate | solution.py:122
  404.4 125.4 %all-reduce.2 = (bf16[13,1024]{1,0:T(8,128)(2,1)}, bf16[1024]{0:T(1024)(128)(2,1)}, bf16[1024,256]{1,0:T(8,128)(2,1)}, bf16[256]{0:T(256)(128)(2,1)}, bf16[256,2...) all-reduce(f32[13,1024]{1,0:T(8,128)S(1)} %fusion.18, ...), channel_id=1, replica_groups=mesh['rep'=16,'mp'=32] {'rep','mp'}, use_global_device_ids=true, to_apply=%region_5.6 | all-reduce | flops 408064 | bytes 2448384 | tf_op jit(solution)/shard_map/psum | solution.py:149
  529.8 109.0 %reduce-scatter.3.cloned.1.call-done = bf16[512,640]{1,0:T(8,128)(2,1)} async-done(((bf16[8192,640]{1,0:T(8,128)(2,1)}), bf16[512,640]{1,0:T(8,128)(2,1)}) %reduce-scatter.3.cloned.1.call-update) | async-done | bytes 655376 | tf_op jit(solution)/shard_map/reduce_scatter | solution.py:148
  638.8 2.3 convert_multiply_fusion.3
  641.1 115.5 %reduce-scatter.5.cloned.1.call-done = f32[16,640]{1,0:T(8,128)} async-done(((f32[512,640]{1,0:T(8,128)}), f32[16,640]{1,0:T(8,128)}) %reduce-scatter.5.cloned.1.call-update) | async-done | bytes 40976 | tf_op jit(solution)/shard_map/reduce_scatter | solution.py:151
  757.3 44.0 %all_gather.11 = bf16[256,640]{1,0:T(8,128)(2,1)S(1)} all-gather(bf16[16,640]{1,0:T(8,128)(2,1)S(1)} %convert_element_type.164), channel_id=1, replica_groups=mesh['rep'=16,'mp'=32] {'rep'}, dimensions={0}, use_global_device_ids=true | all-gather | bytes 348160 | tf_op jit(solution)/shard_map/all_gather | solution.py:155
  (89 shorter events, 22.6 us)
Async XLA Ops:
  7.2 77.8 %copy-start = (bf16[1024,256]{1,0:T(8,128)(2,1)S(1)}, bf16[1024,256]{1,0:T(8,128)(2,1)}, u32[]{:S(2)}) copy-start(bf16[1024,256]{1,0:T(8,128)(2,1)} %param.26) | copy-start | bytes 1572868
  7.2 76.7 %copy-start.16 = (bf16[1024]{0:T(1024)(128)(2,1)S(1)}, bf16[1024]{0:T(1024)(128)(2,1)}, u32[]{:S(2)}) copy-start(bf16[1024]{0:T(1024)(128)(2,1)} %param.25) | copy-start | bytes 6148
  7.2 76.7 %copy-start.17 = (bf16[256]{0:T(256)(128)(2,1)S(1)}, bf16[256]{0:T(256)(128)(2,1)}, u32[]{:S(2)}) copy-start(bf16[256]{0:T(256)(128)(2,1)} %param.27) | copy-start | bytes 1540
  7.2 76.7 %copy-start.18 = (bf16[256]{0:T(256)(128)(2,1)S(1)}, bf16[256]{0:T(256)(128)(2,1)}, u32[]{:S(2)}) copy-start(bf16[256]{0:T(256)(128)(2,1)} %param.23) | copy-start | bytes 1540
  7.2 76.7 %copy-start.15 = (bf16[128,13]{0,1:T(8,128)(2,1)S(1)}, bf16[128,13]{0,1:T(8,128)(2,1)}, u32[]{:S(2)}) copy-start(bf16[128,13]{0,1:T(8,128)(2,1)} %param.15) | copy-start | bytes 9988
  7.2 76.7 %copy-start.14 = (bf16[13,1024]{1,0:T(8,128)(2,1)S(1)}, bf16[13,1024]{1,0:T(8,128)(2,1)}, u32[]{:S(2)}) copy-start(bf16[13,1024]{1,0:T(8,128)(2,1)} %param.24) | copy-start | bytes 79876
  7.2 77.8 %copy-start.11 = (bf16[128,256]{1,0:T(8,128)(2,1)S(1)}, bf16[128,256]{1,0:T(8,128)(2,1)}, u32[]{:S(2)}) copy-start(bf16[128,256]{1,0:T(8,128)(2,1)} %param.29) | copy-start | bytes 196612
  7.3 316.3 %all-gather.2.cloned.1.call-start = ((), (), s32[]{:S(2)}) async-start(), calls=%async_computation.3 | async-start | bytes 11141120 | tf_op jit(solution)/shard_map/all_gather | solution.py:66
  71.0 263.9 %all-to-all-start = ((bf16[32,64,128]{2,1,0:T(8,128)(2,1)}), bf16[32,64,128]{2,1,0:T(8,128)(2,1)S(1)}, u32[]{:S(2)}, u32[]{:S(2)}) async-start(bf16[32,64,128]{2,1,0:T(8,128)(2,1)} %bitcast.72), calls=%async_computation | async-start | bytes 1048576 | tf_op jit(solution)/shard_map/all_to_all | solution.py:72
  83.8 554.9 %reduce-scatter.3.cloned.1.call-start = ((), (), s32[]{:S(2)}) async-start(), calls=%async_computation.4 | async-start | bytes 11141120 | tf_op jit(solution)/shard_map/reduce_scatter | solution.py:148
  335.6 1.3 copy-start.4
  346.1 3.8 copy-start.13
  346.1 3.9 copy-start.2
  350.1 3.5 copy-start.8
  350.1 3.7 copy-start.5
  350.1 11.7 %slice-start = ((s8[10485760]{0:T(1024)(128)(4,1)}), s8[4194304]{0:T(1024)(128)(4,1)S(1)}, s32[]{:S(2)}) async-start(s8[10485760]{0:T(1024)(128)(4,1)} %bitcast.77), calls=%async_computation.6 | async-start | bytes 8388608
  350.1 11.7 %slice-start.1 = ((s8[10485760]{0:T(1024)(128)(4,1)}), s8[4194304]{0:T(1024)(128)(4,1)S(1)}, s32[]{:S(2)}) async-start(s8[10485760]{0:T(1024)(128)(4,1)} %bitcast.77), calls=%async_computation.7 | async-start | bytes 8388608
  353.8 4.1 copy-start.19
  353.8 4.4 copy-start.10
  353.8 8.0 slice-start.2
  375.1 4.8 copy-start.3
  379.9 2.5 copy-start.12
  403.2 401.0 %copy-start.1 = (bf16[1024,256]{1,0:T(8,128)(2,1)S(1)}, bf16[1024,256]{1,0:T(8,128)(2,1)}, u32[]{:S(2)}) copy-start(bf16[1024,256]{1,0:T(8,128)(2,1)} %param.26) | copy-start | bytes 1572868
  403.2 353.4 %reduce-scatter.5.cloned.1.call-start = ((), (), s32[]{:S(2)}) async-start(), calls=%async_computation.5 | async-start | bytes 1351680 | tf_op jit(solution)/shard_map/reduce_scatter | solution.py:151
  (3 other events, 3.3 us)
Sparse Core Ops, SparseCore 0:
  68.7 254.8 all-gather.1
  403.3 235.4 reduce-scatter.2
  643.2 113.3 reduce-scatter.4
